TPU v7x, 32 devices: a whole 2x2x4 slice. The times are simulated.
32 devices in a mesh: row: 4 (over y, x), col: 8 (over z, core).
Axes of the slice: x: 2, y: 2, z: 4, core: 2. Of those that a mesh axis runs over, the one named last changes fastest.
Arguments:
- replay_pool: bfloat16 [4096, 512], P('row'), may hold values from -6 to 6
- sample_ids: int32 [4, 1024], P('row'), may hold values from 0 to 1023, each once within a row
- rotation_bins: int32 [4096], P('row'), may hold values from 0 to 15
Outputs:
- factored: float32 [4096, 4096], P('row', 'col')
Inputs may be any that keep to these rules, and one draw needn't show every extreme that they name: Each row of sample_ids is a permutation of 0 to 1023.
All inputs are finite; a program needn't handle non-finite values.
Results may differ from a plain program's by a relative error of at most 0.0003.
Values may be sent and summed in bfloat16 or wider, within the bound.
No kernel may reach another device: no remote copies, remote signals or barrier semaphores. Data moves between devices by JAX's collectives and lax.ppermute only.
A program may use at most 128 MiB of HBM per device.

v0:
```python
import jax
import jax.numpy as jnp
from jax import lax
from jax.sharding import PartitionSpec as P

ROTS = 16


sharpness = 2.0
ridge_weight = 0.1
highest = lax.Precision.HIGHEST


def from_root(x, axis, root):
    mine = lax.axis_index(axis) == root
    return lax.psum(jnp.where(mine, x, jnp.zeros_like(x)), axis)


def orbit_kernel(row_feats, row_rot, row_global, col_feats, col_rot, col_global):
    feat_width = row_feats.shape[1]
    rotations = ROTS
    row_norms = jnp.sum(jnp.square(row_feats.astype(jnp.float32)), axis=1)
    col_norms = jnp.sum(jnp.square(col_feats.astype(jnp.float32)), axis=1)
    col_binned = col_feats.reshape(col_feats.shape[0], rotations, feat_width // rotations)
    summed = jnp.zeros((row_feats.shape[0], col_feats.shape[0]), jnp.float32)
    for rotation in range(rotations):
        rolled = jnp.roll(col_binned, rotation, axis=1).reshape(col_feats.shape[0], feat_width)
        products = jnp.einsum("nf,mf->nm", row_feats, rolled, preferred_element_type=jnp.float32)
        distance = row_norms[:, None] + col_norms[None, :] - 2.0 * products
        summed = summed + jnp.exp(-distance / feat_width)
    bin_gap = (row_rot[:, None] - col_rot[None, :]).astype(jnp.float32)
    weight = jnp.exp(sharpness * (jnp.cos(bin_gap * (2.0 * jnp.pi / rotations)) - 1.0))
    same_point = (row_global[:, None] == col_global[None, :]).astype(jnp.float32)
    return weight * summed / rotations + ridge_weight * same_point


def per_device(replay_pool, sample_ids, rotation_bins):
    rows_here = lax.axis_size("row")
    cols_here = lax.axis_size("col")
    row_index = lax.axis_index("row")
    column_index = lax.axis_index("col")
    rows_dev = replay_pool.shape[0]
    block_rows = rows_dev // rows_here
    block_cols = rows_dev // cols_here
    cols_dev = block_cols * rows_here
    features = replay_pool[sample_ids[0]]
    col_start = column_index * block_cols
    col_piece = lax.dynamic_slice_in_dim(features, col_start, block_cols, 0)
    col_rot_piece = lax.dynamic_slice_in_dim(rotation_bins, col_start, block_cols, 0)
    col_feats, col_rot = (
        lax.all_gather(col_piece, "row", axis=0, tiled=True),
        lax.all_gather(col_rot_piece, "row", axis=0, tiled=True),
    )
    cycles = jnp.arange(rows_here, dtype=jnp.int32)[:, None]
    col_global = (
        (cycles * cols_here + column_index) * block_cols
        + jnp.arange(block_cols, dtype=jnp.int32)[None, :]
    ).reshape(cols_dev)
    row_global = row_index * rows_dev + jnp.arange(rows_dev, dtype=jnp.int32)
    local_tile = orbit_kernel(features, rotation_bins, row_global, col_feats, col_rot, col_global)
    kernel_tile = lax.all_to_all(local_tile, "row", split_axis=0, concat_axis=0, tiled=True)
    panel_columns = lax.all_gather(kernel_tile[:, :block_cols], "col", axis=1, tiled=True)
    pieces = lax.all_gather(
        kernel_tile[None, :block_rows, :block_cols], ("row", "col"), axis=0, tiled=True
    )
    diag_block = (
        pieces.reshape(rows_here, cols_here, block_rows, block_cols)
        .transpose(0, 2, 1, 3)
        .reshape(rows_dev, rows_dev)
    )
    diag_factor = jnp.linalg.cholesky(diag_block)
    panel = jax.scipy.linalg.solve_triangular(diag_factor, panel_columns.T, lower=True).T
    lead_feats, lead_rot = (from_root(features, "row", 0), from_root(rotation_bins, "row", 0))
    lead_global = jnp.arange(rows_dev, dtype=jnp.int32)
    cross = orbit_kernel(
        col_feats[block_cols:],
        col_rot[block_cols:],
        col_global[block_cols:],
        lead_feats,
        lead_rot,
        lead_global,
    )
    col_panel = jax.scipy.linalg.solve_triangular(diag_factor, cross.T, lower=True).T
    trailing = kernel_tile[:, block_cols:] - jnp.einsum(
        "nk,mk->nm", panel, col_panel, precision=highest
    )
    leading = lax.dynamic_slice_in_dim(panel, col_start, block_cols, 1)
    return jnp.concatenate([leading, trailing], axis=1)


def solution(mesh):
    in_specs = (P("row", None), P("row", None), P("row"))
    out_specs = P("row", "col")
    return jax.shard_map(
        per_device, mesh=mesh, in_specs=in_specs, out_specs=out_specs, check_vma=False
    )
```

profile of v0, /device:TPU:0, one launch (start us, length us, event | category | flops | bytes accessed | tf_op | source)
XLA Modules:
  0.0 564.2 jit_solution(1071801586367604348)
XLA Ops:
  8.6 4.0 gather_fusion
  13.7 14.0 %all_gather.13 = bf16[512,512]{1,0:T(8,128)(2,1)S(1)} all-gather(bf16[128,512]{1,0:T(8,128)(2,1)S(1)} %constant_dynamic-slice_fusion.1), channel_id=1, replica_groups=mesh['row'=4,'col'=8] {'row'}, dimensions={0}, use_global_device_ids=true | all-gather | bytes 655360 | tf_op jit(solution)/shard_map/all_gather | solution.py:51
  56.9 8.5 %all-gather.1 = s32[4,1,128]{2,1,0:T(1,128)S(1)} all-gather(s32[1,1,128]{2,1,0:T(1,128)S(1)} %dynamic-slice_bitcast_fusion.1), channel_id=1, replica_groups=mesh['row'=4,'col'=8] {'row'}, dimensions={0}, use_global_device_ids=true | all-gather | bytes 2560 | tf_op jit(solution)/shard_map/all_gather | solution.py:52
  65.4 15.8 %select_add_fusion = f32[1024,512]{1,0:T(8,128)} fusion(f32[1024,512]{1,0:T(8,128)S(1)} %fusion.307, f32[1024,512]{1,0:T(8,128)S(1)} %fusion.306, f32[1024,512]{1,0:T(8,128)S(1)} %fusion.305, f32[1024,512]{1,0:T(8,128)S(1)} %fusion.304, f32[1024,512]{1,0:T(8,128)S(1)} %fusion.303, f32[1024,512]{1,0:T(8,128)S(1)} %fusion.302, f32[1024,512]{1,0:T(8,128)S(1)} %fusion.301, ...), kind=kOutput, calls=%fused_computation.113 | convolution fusion | flops 584056832 | bytes 35145728 | tf_op jit(solution)/shard_map/nf,mf->nm/dot_general | solution.py:28
  81.2 4.5 all-to-all-start
  85.8 22.7 %psum.14 = s32[1024]{0:T(1024)S(1)} all-reduce(s32[1024]{0:T(1024)S(1)} %broadcast_select_fusion.1), channel_id=1, replica_groups=mesh['row'=4,'col'=8] {'row'}, use_global_device_ids=true, to_apply=%region_18.19 | all-reduce | flops 1024 | bytes 8192 | tf_op jit(solution)/shard_map/psum | solution.py:16
  139.1 13.2 %select_add_fusion.1 = f32[1024,384]{1,0:T(8,128)} fusion(f32[1024,384]{1,0:T(8,128)S(1)} %fusion.232, f32[1024,384]{1,0:T(8,128)S(1)} %fusion.234, f32[1024,384]{1,0:T(8,128)S(1)} %fusion.236, f32[1024,384]{1,0:T(8,128)S(1)} %fusion.238, f32[1024,384]{1,0:T(8,128)S(1)} %fusion.240, f32[1024,384]{1,0:T(8,128)S(1)} %fusion.242, ...), kind=kOutput, calls=%fused_computation.185 | convolution fusion | flops 438042624 | bytes 26621952 | tf_op jit(solution)/shard_map/nf,mf->nm/dot_general | solution.py:28
  157.5 26.3 %all-gather.7.cloned.1.call-done = f32[8192,128]{0,1:T(8,128)} async-done(((f32[256,128]{0,1:T(8,128)}), f32[8192,128]{0,1:T(8,128)}) %all-gather.7.cloned.1.call-update) | async-done | bytes 4194320 | tf_op jit(solution)/shard_map/all_gather | solution.py:63
  183.8 3.5 copy.24
  188.9 3.0 copy.25
  191.9 5.6 copy.17
  197.6 4.5 fusion
  204.1 11.7 %cholesky.223 = f32[128,128]{1,0:T(8,128)S(1)} custom-call(f32[128,128]{1,0:T(8,128)S(1)} %cholesky.580), custom_call_target="Cholesky" | custom-call | tf_op jit(solution)/shard_map/jit(cholesky)/cholesky | solution.py:71
  218.4 9.8 %custom-call.66 = f32[1,128,128]{1,2,0:T(8,128)S(1)} custom-call(f32[1,128,128]{2,1,0:T(8,128)S(1)} %get-tuple-element.154), custom_call_target="InvertDiagBlocksLowerTriangular" | custom-call | tf_op jit(solution)/shard_map/jit(cholesky)/cholesky | solution.py:71
  232.2 12.1 %cholesky.244 = f32[128,128]{1,0:T(8,128)S(1)} custom-call(f32[128,128]{1,0:T(8,128)S(1)} %cholesky.584), custom_call_target="Cholesky" | custom-call | tf_op jit(solution)/shard_map/jit(cholesky)/cholesky | solution.py:71
  244.9 9.8 %custom-call.67 = f32[1,128,128]{1,2,0:T(8,128)S(1)} custom-call(f32[1,128,128]{2,1,0:T(8,128)S(1)} %get-tuple-element.151), custom_call_target="InvertDiagBlocksLowerTriangular" | custom-call | tf_op jit(solution)/shard_map/jit(cholesky)/cholesky | solution.py:71
  258.1 11.7 %cholesky.468 = f32[128,128]{1,0:T(8,128)S(1)} custom-call(f32[128,128]{1,0:T(8,128)S(1)} %cholesky.589), custom_call_target="Cholesky" | custom-call | tf_op jit(solution)/shard_map/jit(cholesky)/cholesky | solution.py:71
  270.5 9.8 %custom-call.68 = f32[1,128,128]{1,2,0:T(8,128)S(1)} custom-call(f32[1,128,128]{2,1,0:T(8,128)S(1)} %get-tuple-element.148), custom_call_target="InvertDiagBlocksLowerTriangular" | custom-call | tf_op jit(solution)/shard_map/jit(cholesky)/cholesky | solution.py:71
  283.8 11.9 %cholesky.487 = f32[128,128]{1,0:T(8,128)S(1)} custom-call(f32[128,128]{1,0:T(8,128)S(1)} %cholesky.594), custom_call_target="Cholesky" | custom-call | tf_op jit(solution)/shard_map/jit(cholesky)/cholesky | solution.py:71
  296.3 9.8 %custom-call.69 = f32[1,128,128]{1,2,0:T(8,128)S(1)} custom-call(f32[1,128,128]{2,1,0:T(8,128)S(1)} %get-tuple-element.145), custom_call_target="InvertDiagBlocksLowerTriangular" | custom-call | tf_op jit(solution)/shard_map/jit(cholesky)/cholesky | solution.py:71
  309.6 11.7 %cholesky.506 = f32[128,128]{1,0:T(8,128)S(1)} custom-call(f32[128,128]{1,0:T(8,128)S(1)} %cholesky.599), custom_call_target="Cholesky" | custom-call | tf_op jit(solution)/shard_map/jit(cholesky)/cholesky | solution.py:71
  321.9 10.0 %custom-call.70 = f32[1,128,128]{1,2,0:T(8,128)S(1)} custom-call(f32[1,128,128]{2,1,0:T(8,128)S(1)} %get-tuple-element.142), custom_call_target="InvertDiagBlocksLowerTriangular" | custom-call | tf_op jit(solution)/shard_map/jit(cholesky)/cholesky | solution.py:71
  335.2 11.7 %cholesky.526 = f32[128,128]{1,0:T(8,128)S(1)} custom-call(f32[128,128]{1,0:T(8,128)S(1)} %cholesky.604), custom_call_target="Cholesky" | custom-call | tf_op jit(solution)/shard_map/jit(cholesky)/cholesky | solution.py:71
  347.5 9.8 %custom-call.71 = f32[1,128,128]{1,2,0:T(8,128)S(1)} custom-call(f32[1,128,128]{2,1,0:T(8,128)S(1)} %get-tuple-element.139), custom_call_target="InvertDiagBlocksLowerTriangular" | custom-call | tf_op jit(solution)/shard_map/jit(cholesky)/cholesky | solution.py:71
  360.4 11.7 %cholesky.546 = f32[128,128]{1,0:T(8,128)S(1)} custom-call(f32[128,128]{1,0:T(8,128)S(1)} %cholesky.609), custom_call_target="Cholesky" | custom-call | tf_op jit(solution)/shard_map/jit(cholesky)/cholesky | solution.py:71
  372.7 9.8 %custom-call.72 = f32[1,128,128]{1,2,0:T(8,128)S(1)} custom-call(f32[1,128,128]{2,1,0:T(8,128)S(1)} %get-tuple-element.136), custom_call_target="InvertDiagBlocksLowerTriangular" | custom-call | tf_op jit(solution)/shard_map/jit(cholesky)/cholesky | solution.py:71
  385.2 11.7 %cholesky.564 = f32[128,128]{1,0:T(8,128)S(1)} custom-call(f32[128,128]{1,0:T(8,128)S(1)} %convolution_subtract_fusion.19), custom_call_target="Cholesky" | custom-call | tf_op jit(solution)/shard_map/jit(cholesky)/cholesky | solution.py:71
  408.7 4.9 select_select_fusion
  413.6 28.7 %while.1 = (s32[]{:T(128)}, f32[1024,1024]{1,0:T(8,128)}, s32[8,2]{0,1:T(2,128)S(1)}, f32[8,128,128]{2,1,0:T(8,128)}, s32[]{:T(128)}) while((s32[]{:T(128)}, f32[1024,1024]{1,0:T(8,128)}, s32[8,2]{0,1:T(2,128)S(1)}, f32[8,128,128]{2,1,0:T(8,128)}, s32[]{:T(128)}) %tuple.121), condition=%wide.while_cond, body=%wide.while_body.sunk | while | flops 2 | bytes 132205 | solution.py:72
  414.2 2.9 bitcast_dynamic-update-slice_fusion.2
  442.3 79.6 %custom-call.73 = f32[8,128,128]{1,2,0:T(8,128)S(1)} custom-call(f32[8,128,128]{2,1,0:T(8,128)} %get-tuple-element.12), custom_call_target="InvertDiagBlocksLowerTriangular" | custom-call | tf_op jit(solution)/shard_map/jit(_solve_triangular)/triangular_solve | solution.py:72
  548.7 5.6 convolution_subtract_fusion
  (296 shorter events, 160.7 us)
Async XLA Ops:
  7.4 1.2 copy-start
  7.4 101.8 %all-reduce.3.cloned.1.call-start = ((), (), s32[]{:S(2)}) async-start(), calls=%async_computation.2 | async-start | bytes 2097152 | tf_op jit(solution)/shard_map/psum | solution.py:16
  43.4 1.1 copy-start.18
  43.4 1.1 copy-start.38
  43.4 1.2 copy-start.39
  44.7 1.1 copy-start.36
  44.7 1.2 copy-start.37
  46.0 1.2 copy-start.35
  47.3 1.2 copy-start.33
  48.6 1.2 copy-start.31
  56.0 9.3 %copy-start.40 = (bf16[512,1,32]{0,2,1:T(8,128)(2,1)S(1)}, bf16[512,1,32]{0,2,1:T(8,128)(2,1)}, u32[]{:S(2)}) copy-start(bf16[512,1,32]{0,2,1:T(8,128)(2,1)} %get-tuple-element.80) | copy-start | bytes 98308
  56.0 9.4 %copy-start.16 = (f32[1024,512]{1,0:T(8,128)S(1)}, f32[1024,512]{1,0:T(8,128)}, u32[]{:S(2)}) copy-start(f32[1024,512]{1,0:T(8,128)} %fusion.293) | copy-start | bytes 6291460
  81.2 38.5 %all-to-all-start = ((f32[4,256,512]{2,1,0:T(8,128)}), f32[4,256,512]{2,1,0:T(8,128)}, u32[]{:S(2)}, u32[]{:S(2)}) async-start(f32[4,256,512]{2,1,0:T(8,128)} %bitcast.302), calls=%async_computation | async-start | bytes 4194304 | tf_op jit(solution)/shard_map/all_to_all | solution.py:61
  85.7 98.1 %all-gather.7.cloned.1.call-start = ((), (), s32[]{:S(2)}) async-start(), calls=%async_computation.3 | async-start | bytes 4325376 | tf_op jit(solution)/shard_map/all_gather | solution.py:63
  121.4 400.5 %all-gather.5.cloned.1.call-start = ((), (), s32[]{:S(2)}) async-start(), calls=%async_computation.1 | async-start | bytes 4718592 | tf_op jit(solution)/shard_map/all_gather | solution.py:62
  121.9 1.4 copy-start.14
  121.9 1.6 copy-start.15
  124.3 1.2 copy-start.4
  124.3 1.5 copy-start.9
  125.5 1.3 copy-start.11
  126.6 1.3 copy-start.12
  130.1 1.2 copy-start.6
  133.6 1.2 copy-start.10
  134.4 1.3 copy-start.8
  135.6 1.2 copy-start.7
  202.1 2.0 copy-start.3
  408.7 4.9 copy-start.43
  523.7 2.6 copy-start.2
  526.2 2.7 copy-start.13
  537.6 2.5 copy-start.25
  546.5 2.2 copy-start.5
  554.3 2.1 copy-start.1
  (16 other events, 16.1 us)
Sparse Core Ops, SparseCore 0:
  13.8 56.5 all-reduce.2
Sparse Core Ops, SparseCore 1:
  121.5 62.2 all-gather.6
  185.3 44.9 all-gather.4
where the time goes:
time: 572 us; the launch traced here: 564 us
  other arithmetic  275 us (48%)
  matrix products  107 us (19%)
  local copies, waits for them, and re-layouts  83.2 us (15%)
  blocking collectives  45.2 us (8%)
  waiting for transfers between devices  26.4 us (5%)
  between operations  22 us (4%)
    another operation x31, other arithmetic, per_device(): diag_factor = jnp.linalg.cholesky(diag_block)  173 us
    another operation x3, other arithmetic, per_device(): jax.scipy.linalg.solve_triangular(diag_factor, panel_columns.T, lower=True)  84.9 us
    dot_general x32, matrix products, orbit_kernel(): jnp.einsum('nf,mf->nm', row_feats, rolled, preferred_element_type=jnp.flo...  52.1 us
    another operation x24, local copies, waits for them, and re-layouts  28.7 us
    all_gather x1, waiting for transfers between devices, per_device(): lax.all_gather(kernel_tile[None, :block_rows, :block_cols], ('row', 'col'...  26.3 us
    another operation x14, matrix products, per_device(): diag_factor = jnp.linalg.cholesky(diag_block)  23 us
    psum x1, blocking collectives, from_root(): return lax.psum(jnp.where(mine, x, jnp.zeros_like(x)), axis)  22.7 us
    another operation x15, matrix products, per_device(): jax.scipy.linalg.solve_triangular(diag_factor, panel_columns.T, lower=True)  18.7 us
  transfers between devices with their start and end apart: 4, of which 1 were waited for; matrix products, arithmetic and copies ran while one was open for 74% of the time, Pallas kernels for 0%

commit v1 on v0

v1 whole, which is shorter than its diff:
```python
import functools

import jax
import jax.numpy as jnp
import numpy as np
from jax import lax
from jax.experimental import pallas as pl
from jax.experimental.pallas import tpu as pltpu
from jax.sharding import PartitionSpec as P

ROTS = 16
SHARPNESS = 2.0
RIDGE = 0.1
BIG = 256
SMALL = 128
F32, BF16 = jnp.float32, jnp.bfloat16


def split(x):
    hi = x.astype(BF16)
    return hi, (x - hi.astype(F32)).astype(BF16)


def dot_nt(a, b):
    return lax.dot_general(a, b, (((1,), (1,)), ((), ())), preferred_element_type=F32)


def dot_nn(a, b):
    return jnp.dot(a, b, preferred_element_type=F32)


def dot3(dot, ah, al, bh, bl):
    return dot(ah, bh) + (dot(ah, bl) + dot(al, bh))


def gauss_jordan(rows):
    groups = len(rows)
    shape = (8, SMALL)
    sub = lax.broadcasted_iota(jnp.int32, shape, 0)
    lane = lax.broadcasted_iota(jnp.int32, shape, 1)
    left = list(rows)
    right = [jnp.where(sub + 8 * g == lane, 1.0, 0.0).astype(F32) for g in range(groups)]
    out = []
    for g in range(groups):
        a, b = left[g], right[g]
        cols = [jnp.broadcast_to(a[:, 8 * g + k : 8 * g + k + 1], shape) for k in range(8)]
        kept = jnp.zeros(shape, F32)
        for k in range(8):
            pivot = jnp.broadcast_to(cols[k][k : k + 1, :], shape)
            inv = 1.0 / pivot
            mult = jnp.where(sub == k, 1.0 - inv, cols[k] * inv)
            arow = jnp.broadcast_to(a[k : k + 1, :], shape)
            brow = jnp.broadcast_to(b[k : k + 1, :], shape)
            kept = jnp.where(sub == k, brow * lax.rsqrt(pivot), kept)
            a = a - mult * arow
            b = b - mult * brow
            for j in range(k + 1, 8):
                cols[j] = cols[j] - mult * jnp.broadcast_to(cols[j][k : k + 1, :], shape)
        out.append(kept)
        for i in range(g + 1, groups):
            suma = sumb = None
            for k in range(8):
                c = jnp.broadcast_to(left[i][:, 8 * g + k : 8 * g + k + 1], shape)
                ta = c * jnp.broadcast_to(a[k : k + 1, :], shape)
                tb = c * jnp.broadcast_to(b[k : k + 1, :], shape)
                suma, sumb = (ta, tb) if suma is None else (suma + ta, sumb + tb)
            left[i] = left[i] - suma
            right[i] = right[i] - sumb
    return out


def mega_kernel(dims, pq_ref, x_ref, lt_ref, ct_ref, xi_ref, li_ref, ci_ref, *refs):
    lead, other, block_rows, rows_other, tile_other, width = dims
    trail_out, *refs = refs
    if width is None:
        lead_out, *refs = refs
    s_ref, ph_ref, pl_ref, d_ref, x32_ref, ln_ref, cn_ref = refs
    feat = x_ref.shape[1]
    chan = feat // ROTS
    nbig = lead // BIG
    cols_pad = ct_ref.shape[1]

    def evaluate(row0, tm, t_ref, info_ref, norm_ref, col0, tn):
        a = x_ref[pl.ds(row0, tm), :]
        acc = None
        for s in range(ROTS):
            w = t_ref[feat - chan * s : 2 * feat - chan * s, pl.ds(col0, tn)]
            e = jnp.exp(dot_nn(a, w))
            acc = e if acc is None else acc + e
        af = a.astype(F32)
        rn = jnp.sum(af * af, axis=1, keepdims=True) * (1.0 / feat)
        info = xi_ref[pl.ds(row0, tm), :]
        rc, rs, rg = info[:, 0:1], info[:, 1:2], info[:, 2:3]
        cc, cs, cg = (info_ref[k : k + 1, pl.ds(col0, tn)] for k in range(3))
        cn = norm_ref[0:1, pl.ds(col0, tn)]
        arg = (2.0 * rc) * cc + (2.0 * rs) * cs - (rn + SHARPNESS) - cn
        value = acc * jnp.exp(arg) * (1.0 / ROTS)
        return value + jnp.where(rg == cg, RIDGE, 0.0).astype(F32)

    def al(v, m):
        return pl.multiple_of(v, m)

    for t_ref, norm_ref in ((lt_ref, ln_ref), (ct_ref, cn_ref)):
        t = t_ref[0:feat, :].astype(F32)
        norm_ref[0:1, :] = jnp.sum(t * t, axis=0, keepdims=True) * (256.0 * 256.0 / feat)

    def lead_col(j, _):
        def lead_row(i, _):
            r0, c0 = al(i * BIG, BIG), al(j * BIG, BIG)
            s_ref[pl.ds(r0, BIG), pl.ds(c0, BIG)] = evaluate(r0, BIG, lt_ref, li_ref, ln_ref, c0, BIG)
            return 0
        lax.fori_loop(j, nbig, lead_row, 0)
        def upper_row(i, _):
            r0, c0 = al(i * BIG, BIG), al(j * BIG, BIG)
            s_ref[pl.ds(r0, BIG), pl.ds(c0, BIG)] = jnp.zeros((BIG, BIG), F32)
            ph_ref[pl.ds(r0, BIG), pl.ds(c0, BIG)] = jnp.zeros((BIG, BIG), BF16)
            pl_ref[pl.ds(r0, BIG), pl.ds(c0, BIG)] = jnp.zeros((BIG, BIG), BF16)
            return 0
        lax.fori_loop(0, j, upper_row, 0)
        def other_row(i, _):
            r0, c0 = al(lead + i * tile_other, SMALL), al(j * BIG, BIG)
            s_ref[pl.ds(r0, tile_other), pl.ds(c0, BIG)] = evaluate(r0, tile_other, lt_ref, li_ref, ln_ref, c0, BIG)
            return 0
        lax.fori_loop(0, other // tile_other, other_row, 0)
        return 0
    lax.fori_loop(0, nbig, lead_col, 0)

    def invert(r0):
        rows = [d_ref[r0 + 8 * g : r0 + 8 * g + 8, r0 : r0 + SMALL] for g in range(SMALL // 8)]
        for g, v in enumerate(gauss_jordan(rows)):
            x32_ref[r0 + 8 * g : r0 + 8 * g + 8, r0 : r0 + SMALL] = v

    def big_step(j, _):
        c0 = al(j * BIG, BIG)
        cj = pl.ds(c0, BIG)
        d_ref[...] = s_ref[cj, cj]
        invert(0)
        x11 = split(x32_ref[0:SMALL, 0:SMALL])
        l21 = dot3(dot_nt, *split(d_ref[SMALL:, 0:SMALL]), *x11)
        l21s = split(l21)
        d_ref[SMALL:, SMALL:] = d_ref[SMALL:, SMALL:] - dot3(dot_nt, *l21s, *l21s)
        invert(SMALL)
        x22 = split(x32_ref[SMALL:, SMALL:])
        mid = split(dot3(dot_nn, *l21s, *x11))
        x32_ref[SMALL:, 0:SMALL] = -dot3(dot_nn, *x22, *mid)
        x32_ref[0:SMALL, SMALL:] = jnp.zeros((SMALL, SMALL), F32)
        xh, xl = split(x32_ref[...])

        def solve(r0, tm, mask):
            v = dot3(dot_nt, *split(s_ref[pl.ds(r0, tm), cj]), xh, xl)
            if mask:
                keep = lax.broadcasted_iota(jnp.int32, v.shape, 0) >= lax.broadcasted_iota(jnp.int32, v.shape, 1)
                v = jnp.where(keep, v, 0.0)
            s_ref[pl.ds(r0, tm), cj] = v
            h, l = split(v)
            ph_ref[pl.ds(r0, tm), cj] = h
            pl_ref[pl.ds(r0, tm), cj] = l

        solve(c0, BIG, True)
        def lead_solve(i, _):
            solve(al(i * BIG, BIG), BIG, False)
            return 0
        lax.fori_loop(j + 1, nbig, lead_solve, 0)
        def other_solve(i, _):
            solve(al(lead + i * tile_other, SMALL), tile_other, False)
            return 0
        lax.fori_loop(0, other // tile_other, other_solve, 0)

        def update(r0, tm, k0):
            kj = pl.ds(k0, BIG)
            rows = pl.ds(r0, tm)
            s_ref[rows, kj] = s_ref[rows, kj] - dot3(
                dot_nt, ph_ref[rows, cj], pl_ref[rows, cj], ph_ref[kj, cj], pl_ref[kj, cj])

        def update_col(k, _):
            k0 = al(k * BIG, BIG)
            def lead_update(i, _):
                update(al(i * BIG, BIG), BIG, k0)
                return 0
            lax.fori_loop(k, nbig, lead_update, 0)
            def other_update(i, _):
                update(al(lead + i * tile_other, SMALL), tile_other, k0)
                return 0
            lax.fori_loop(0, other // tile_other, other_update, 0)
            return 0
        lax.fori_loop(j + 1, nbig, update_col, 0)
        return 0
    lax.fori_loop(0, nbig, big_step, 0)

    first = al(pq_ref[0] * block_rows, block_rows)
    cols0 = lead + rows_other
    groups = 1 + rows_other // block_rows

    def trailing(c, _):
        r0 = al(jnp.where(c == 0, first, lead + (c - 1) * block_rows), SMALL)
        rows = pl.ds(r0, block_rows)
        o0 = al(c * block_rows, block_rows)
        v = evaluate(r0, block_rows, ct_ref, ci_ref, cn_ref, 0, cols_pad)
        v = v - dot3(dot_nt, ph_ref[rows, :], pl_ref[rows, :],
                     ph_ref[cols0 : cols0 + cols_pad, :], pl_ref[cols0 : cols0 + cols_pad, :])
        if width is None:
            lead_out[pl.ds(o0, block_rows), :] = s_ref[rows, :]
            trail_out[pl.ds(o0, block_rows), :] = v
        else:
            q0 = al(pq_ref[1] * width, width)
            trail_out[pl.ds(o0, block_rows), 0:width] = s_ref[rows, pl.ds(q0, width)]
            trail_out[pl.ds(o0, block_rows), width:] = v
        return 0
    lax.fori_loop(0, groups, trailing, 0)


def per_device(replay_pool, sample_ids, rotation_bins):
    rows_n = lax.axis_size("row")
    cols_n = lax.axis_size("col")
    p = lax.axis_index("row")
    q = lax.axis_index("col")
    lead, feat = replay_pool.shape
    block_rows = lead // rows_n
    block_cols = lead // cols_n
    rows_other = (rows_n - 1) * block_rows
    cols_other = (rows_n - 1) * block_cols
    cols_pad = -(-cols_other // SMALL) * SMALL
    other = rows_other + cols_pad
    tile_other = max(t for t in range(SMALL, 513, SMALL) if other % t == 0)
    aligned = block_cols % SMALL == 0

    features = replay_pool[sample_ids[0]]
    bins = rotation_bins.astype(BF16)

    def trailer(values):
        flat = jnp.concatenate(values)
        return jnp.pad(flat, (0, 16 * feat - flat.shape[0])).reshape(16, feat)

    half = lead // 2
    h0 = (q % 2) * half
    message = jnp.concatenate(
        [lax.dynamic_slice_in_dim(features, h0, half, 0), trailer([lax.dynamic_slice_in_dim(bins, h0, half, 0)])])
    mine = jnp.where(p == 0, message, jnp.zeros_like(message))
    for d in range(1, rows_n):
        mine = mine + lax.ppermute(message, "row", [(0, d)])
    theirs = lax.ppermute(mine, "col", [(i, i ^ 1) for i in range(cols_n)])
    even = q % 2 == 0
    low, high = jnp.where(even, mine, theirs), jnp.where(even, theirs, mine)
    lead_feats = jnp.concatenate([low[:half], high[:half]])
    lead_bins = jnp.concatenate([low[half:].reshape(-1)[:half], high[half:].reshape(-1)[:half]])

    c0 = q * block_cols
    col_piece = lax.dynamic_slice_in_dim(features, c0, block_cols, 0)
    col_bins = lax.dynamic_slice_in_dim(bins, c0, block_cols, 0)
    out = jnp.concatenate([
        features.reshape(rows_n, block_rows, feat),
        jnp.broadcast_to(col_piece[None], (rows_n, block_cols, feat)),
        jnp.stack([trailer([bins[r * block_rows : (r + 1) * block_rows], col_bins]) for r in range(rows_n)]),
    ], axis=1)
    got = lax.all_to_all(out, "row", split_axis=0, concat_axis=0)
    row_feats = got[1:, :block_rows].reshape(rows_other, feat)
    col_feats = got[1:, block_rows : block_rows + block_cols].reshape(cols_other, feat)
    tails = got[1:, block_rows + block_cols :].reshape(rows_n - 1, -1)
    row_bins = tails[:, :block_rows].reshape(-1)
    col_bins = tails[:, block_rows : block_rows + block_cols].reshape(-1)
    groups = jnp.arange(1, rows_n, dtype=jnp.int32)[:, None] * lead
    row_ids = (groups + p * block_rows + jnp.arange(block_rows, dtype=jnp.int32)[None]).reshape(-1)
    col_ids = (groups + c0 + jnp.arange(block_cols, dtype=jnp.int32)[None]).reshape(-1)
    extra = cols_pad - cols_other
    col_feats = jnp.pad(col_feats, ((0, extra), (0, 0)))
    col_bins = jnp.pad(col_bins, (0, extra))
    col_ids = jnp.pad(col_ids, (0, extra), constant_values=-1)

    x = jnp.concatenate([lead_feats, row_feats, col_feats])
    angle = jnp.concatenate([lead_bins, row_bins, col_bins]).astype(F32) * (2.0 * np.pi / ROTS)
    ids = jnp.concatenate([jnp.arange(lead, dtype=jnp.int32), row_ids, col_ids]).astype(F32)
    info = jnp.stack([jnp.cos(angle), jnp.sin(angle), ids, jnp.zeros_like(ids)], axis=0)
    xi = info.T
    pad = jnp.zeros((4, info.shape[1]), F32)
    info = jnp.concatenate([info, pad])
    lt = lead_feats.T * BF16(1.0 / 256.0)
    ct = col_feats.T * BF16(1.0 / 256.0)
    lt = jnp.concatenate([lt, lt])
    ct = jnp.concatenate([ct, ct])
    pq = jnp.stack([p, q]).astype(jnp.int32)

    total = lead + other
    dims = (lead, other, block_rows, rows_other, tile_other, block_cols if aligned else None)
    own = rows_n * block_rows
    trail_width = cols_pad + (block_cols if aligned else 0)
    shapes = [jax.ShapeDtypeStruct((own, trail_width), F32)]
    if not aligned:
        shapes.append(jax.ShapeDtypeStruct((own, lead), F32))
    vmem = pl.BlockSpec(memory_space=pltpu.VMEM)
    tile, *lead_out = pl.pallas_call(
        functools.partial(mega_kernel, dims),
        out_shape=shapes,
        in_specs=[pl.BlockSpec(memory_space=pltpu.SMEM)] + [vmem] * 6,
        out_specs=[vmem] * len(shapes),
        scratch_shapes=[
            pltpu.VMEM((total, lead), F32),
            pltpu.VMEM((total, lead), BF16),
            pltpu.VMEM((total, lead), BF16),
            pltpu.VMEM((BIG, BIG), F32),
            pltpu.VMEM((BIG, BIG), F32),
            pltpu.VMEM((8, lead), F32),
            pltpu.VMEM((8, cols_pad), F32),
        ],
        compiler_params=pltpu.CompilerParams(vmem_limit_bytes=56 * 2**20),
        name="panel",
    )(pq, x, lt, ct, xi, info[:, :lead], info[:, lead + rows_other :])
    if aligned:
        return tile
    leading = lax.dynamic_slice_in_dim(lead_out[0], c0, block_cols, 1)
    return jnp.concatenate([leading, tile[:, :cols_other]], axis=1)


def solution(mesh):
    in_specs = (P("row", None), P("row", None), P("row"))
    return jax.shard_map(per_device, mesh=mesh, in_specs=in_specs, out_specs=P("row", "col"), check_vma=False)
```

time: 572 us -> 176 us (0.31); the launches traced: 564 us -> 175 us
  other arithmetic: 275 us -> 8.67 us
  Pallas kernels: 0 us -> 113 us
  matrix products: 107 us -> 0 us
  local copies, waits for them, and re-layouts: 83.2 us -> 14.9 us
  blocking collectives: 45.2 us -> 0 us
  between operations: 22 us -> 0.32 us
  starting transfers between devices: 4.95 us -> 14.3 us
    another operation x34 -> x1, other arithmetic: 258 us -> 0.66 us  [per_device(): pq = jnp.stack([p, q]).astype(jnp.int32)]
    pallas_call x0 -> x1, Pallas kernels: none -> 113 us  [per_device(): pl.pallas_call(functools.partial(mega_kernel, dims), out_shape=shapes, in...]
    dot_general x33 -> x0, matrix products: 57.7 us -> none  [the longest x32 52.1 us: orbit_kernel(): jnp.einsum('nf,mf->nm', row_feats, rolled, preferred_element_type=jnp.flo...]
    another operation x44 -> x0, matrix products: 49.5 us -> none  [the longest x14 23 us: per_device(): diag_factor = jnp.linalg.cholesky(diag_block)]
    another operation x33 -> x5, local copies, waits for them, and re-layouts: 31.3 us -> 0.1 us  [the longest x4 0.09 us: per_device(): jnp.stack([trailer([bins[r * block_rows:(r + 1) * block_rows], col_bins])...]
    all_gather x2 -> x0, waiting for transfers between devices: 26.3 us -> none  [the longest x1 26.3 us: per_device(): lax.all_gather(kernel_tile[None, :block_rows, :block_cols], ('row', 'col'...]
    psum x1 -> x0, blocking collectives: 22.7 us -> none  [from_root(): return lax.psum(jnp.where(mine, x, jnp.zeros_like(x)), axis)]
    all_gather x2 -> x0, blocking collectives: 22.5 us -> none  [the longest x1 14 us: per_device(): lax.all_gather(col_piece, 'row', axis=0, tiled=True)]
  transfers between devices with their start and end apart: 4 -> 5, of which waited for: 1 -> 5; matrix products, arithmetic and copies ran while one was open for 74% -> 4% of each run, Pallas kernels for 0% -> 0%
where the time goes in v1:
time: 176 us; the launch traced here: 175 us
  Pallas kernels  113 us (64%)
  waiting for transfers between devices  24.5 us (14%)
  local copies, waits for them, and re-layouts  14.9 us (8%)
  starting transfers between devices  14.3 us (8%)
  other arithmetic  8.67 us (5%)
    pallas_call x1, Pallas kernels, per_device(): pl.pallas_call(functools.partial(mega_kernel, dims), out_shape=shapes, in...  113 us
    ppermute x3, waiting for transfers between devices, per_device(): mine = mine + lax.ppermute(message, 'row', [(0, d)])  15.3 us
    ppermute x3, starting transfers between devices, per_device(): mine = mine + lax.ppermute(message, 'row', [(0, d)])  9.91 us
    all_to_all x1, waiting for transfers between devices, per_device(): got = lax.all_to_all(out, 'row', split_axis=0, concat_axis=0)  8.04 us
    all_to_all x1, starting transfers between devices, per_device(): got = lax.all_to_all(out, 'row', split_axis=0, concat_axis=0)  4.36 us
    gather x1, local copies, waits for them, and re-layouts, per_device(): features = replay_pool[sample_ids[0]]  3.97 us
  transfers between devices with their start and end apart: 5, of which 5 were waited for; matrix products, arithmetic and copies ran while one was open for 4% of the time, Pallas kernels for 0%

profile of v1, /device:TPU:0, one launch (start us, length us, event | category | flops | bytes accessed | tf_op | source)
XLA Modules:
  0.0 175.5 jit_solution(2561984738183279718)
XLA Ops:
  0.0 0.8 convert_element_type.34
  0.8 0.7 compare_select_fusion
  1.6 4.0 %gather_fusion = bf16[1024,512]{1,0:T(8,128)(2,1)S(1)} fusion(bf16[1024,512]{1,0:T(8,128)(2,1)S(1)} %copy-done, s32[1024]{0:T(1024)S(1)} %broadcast_clamp_fusion), kind=kCustom, calls=%fused_computation | custom fusion | bytes 2101248 | tf_op jit(solution)/shard_map/gather | solution.py:227
  5.7 5.7 %collective-permute-start.1 = (bf16[528,512]{1,0:T(8,128)(2,1)S(1)}, bf16[528,512]{1,0:T(8,128)(2,1)}, u32[]{:S(2)}, u32[]{:S(2)}) collective-permute-start(bf16[528,512]{1,0:T(8,128)(2,1)S(1)} %pad_maximum_fusion.3), channel_id=1, source_target_pairs={{0,16},{1,17},{2,18},{3,19},{4,20},{5,21},{6,22},{7,23}} | collective-permute-start | bytes 1622024 | tf_op jit(solution)/shard_map/ppermute | solution.py:240
  11.4 2.1 %collective-permute-start = (bf16[528,512]{1,0:T(8,128)(2,1)S(1)}, bf16[528,512]{1,0:T(8,128)(2,1)}, u32[]{:S(2)}, u32[]{:S(2)}) collective-permute-start(bf16[528,512]{1,0:T(8,128)(2,1)S(1)} %pad_maximum_fusion.3), channel_id=1, source_target_pairs={{0,8},{1,9},{2,10},{3,11},{4,12},{5,13},{6,14},{7,15}} | collective-permute-start | bytes 1622024 | tf_op jit(solution)/shard_map/ppermute | solution.py:240
  13.5 2.1 %collective-permute-start.2 = (bf16[528,512]{1,0:T(8,128)(2,1)S(1)}, bf16[528,512]{1,0:T(8,128)(2,1)}, u32[]{:S(2)}, u32[]{:S(2)}) collective-permute-start(bf16[528,512]{1,0:T(8,128)(2,1)S(1)} %pad_maximum_fusion.3), channel_id=1, source_target_pairs={{0,24},{1,25},{2,26},{3,27},{4,28},{5,29},{6,30},{7,31}} | collective-permute-start | bytes 1622024 | tf_op jit(solution)/shard_map/ppermute | solution.py:240
  15.9 1.3 maximum_maximum_fusion
  17.2 4.4 %all-to-all-start = ((bf16[4,400,512]{2,1,0:T(8,128)(2,1)}), bf16[4,400,512]{2,1,0:T(8,128)(2,1)}, u32[]{:S(2)}, u32[]{:S(2)}) async-start(bf16[4,400,512]{2,1,0:T(8,128)(2,1)} %maximum_maximum_fusion), calls=%async_computation | async-start | bytes 3276800 | tf_op jit(solution)/shard_map/all_to_all | solution.py:255
  21.7 0.8 collective-permute-done.1
  22.5 2.9 %collective-permute-done = bf16[528,512]{1,0:T(8,128)(2,1)} collective-permute-done((bf16[528,512]{1,0:T(8,128)(2,1)S(1)}, bf16[528,512]{1,0:T(8,128)(2,1)}, u32[]{:S(2)}, u32[]{:S(2)}) %collective-permute-start) | collective-permute-done | bytes 540704 | tf_op jit(solution)/shard_map/ppermute | solution.py:240
  25.3 11.6 %collective-permute-done.2 = bf16[528,512]{1,0:T(8,128)(2,1)} collective-permute-done((bf16[528,512]{1,0:T(8,128)(2,1)S(1)}, bf16[528,512]{1,0:T(8,128)(2,1)}, u32[]{:S(2)}, u32[]{:S(2)}) %collective-permute-start.2) | collective-permute-done | bytes 540704 | tf_op jit(solution)/shard_map/ppermute | solution.py:240
  37.0 1.7 add_add_fusion
  38.8 0.7 pad_add_fusion.pq_ref
  39.5 1.2 collective-permute-done.3
  40.8 0.7 copy-done.1
  41.6 0.8 copy-done.3
  42.4 0.2 fusion
  42.6 0.2 pad_maximum_fusion.1
  42.9 2.6 %copy.12.lt_ref = bf16[1024,1024]{1,0:T(8,128)(2,1)} copy(bf16[1024,1024]{0,1:T(8,128)(2,1)S(1)} %pad_maximum_fusion.1) | data formatting | bytes 4194304 | tf_op jit(solution)/shard_map/concatenate | solution.py:278
  45.4 8.0 %all-to-all-done = bf16[4,400,512]{2,1,0:T(8,128)(2,1)} async-done(((bf16[4,400,512]{2,1,0:T(8,128)(2,1)}), bf16[4,400,512]{2,1,0:T(8,128)(2,1)}, u32[]{:S(2)}, u32[]{:S(2)}) %all-to-all-start) | async-done | bytes 1638432 | tf_op jit(solution)/shard_map/all_to_all | solution.py:255
  53.5 0.8 slice_bitcast_fusion
  54.4 0.2 fusion.4
  54.6 0.2 sin.10
  55.0 0.6 slice.78.ci_ref
  55.6 0.6 slice.77.li_ref
  56.2 1.0 slice.71
  57.3 0.2 copy.11
  57.5 1.2 slice.70
  58.7 1.5 pad_maximum_fusion.x_ref
  60.3 1.0 pad_maximum_fusion.2.ct_ref
  61.2 1.4 copy.13.xi_ref
  62.6 112.9 %panel.1 = f32[1024,512]{1,0:T(8,128)} custom-call(s32[2]{0:T(128)} %pad_add_fusion.pq_ref, bf16[2176,512]{1,0:T(8,128)(2,1)} %pad_maximum_fusion.x_ref, bf16[1024,1024]{1,0:T(8,128)(2,1)} %copy.12.lt_ref, bf16[1024,384]{1,0:T(8,128)(2,1)} %pad_maximum_fusion.2.ct_ref, f32[2176,4]{1,0:T(8,128)} %copy.13.xi_ref, f32[8,1024]{1,0:T(8,128)} %slice.77.li_ref, ...), custom_call_target="tpu_custom_call" | custom-call | tf_op jit(solution)/shard_map/panel/pallas_call | solution.py:290
  (51 shorter events, 1.1 us)
Async XLA Ops:
  0.0 1.6 copy-start
  5.7 16.8 %collective-permute-start.1 = (bf16[528,512]{1,0:T(8,128)(2,1)S(1)}, bf16[528,512]{1,0:T(8,128)(2,1)}, u32[]{:S(2)}, u32[]{:S(2)}) collective-permute-start(bf16[528,512]{1,0:T(8,128)(2,1)S(1)} %pad_maximum_fusion.3), channel_id=1, source_target_pairs={{0,16},{1,17},{2,18},{3,19},{4,20},{5,21},{6,22},{7,23}} | collective-permute-start | bytes 1622024 | tf_op jit(solution)/shard_map/ppermute | solution.py:240
  11.4 13.9 %collective-permute-start = (bf16[528,512]{1,0:T(8,128)(2,1)S(1)}, bf16[528,512]{1,0:T(8,128)(2,1)}, u32[]{:S(2)}, u32[]{:S(2)}) collective-permute-start(bf16[528,512]{1,0:T(8,128)(2,1)S(1)} %pad_maximum_fusion.3), channel_id=1, source_target_pairs={{0,8},{1,9},{2,10},{3,11},{4,12},{5,13},{6,14},{7,15}} | collective-permute-start | bytes 1622024 | tf_op jit(solution)/shard_map/ppermute | solution.py:240
  13.5 23.5 %collective-permute-start.2 = (bf16[528,512]{1,0:T(8,128)(2,1)S(1)}, bf16[528,512]{1,0:T(8,128)(2,1)}, u32[]{:S(2)}, u32[]{:S(2)}) collective-permute-start(bf16[528,512]{1,0:T(8,128)(2,1)S(1)} %pad_maximum_fusion.3), channel_id=1, source_target_pairs={{0,24},{1,25},{2,26},{3,27},{4,28},{5,29},{6,30},{7,31}} | collective-permute-start | bytes 1622024 | tf_op jit(solution)/shard_map/ppermute | solution.py:240
  17.2 36.3 %all-to-all-start = ((bf16[4,400,512]{2,1,0:T(8,128)(2,1)}), bf16[4,400,512]{2,1,0:T(8,128)(2,1)}, u32[]{:S(2)}, u32[]{:S(2)}) async-start(bf16[4,400,512]{2,1,0:T(8,128)(2,1)} %maximum_maximum_fusion), calls=%async_computation | async-start | bytes 3276800 | tf_op jit(solution)/shard_map/all_to_all | solution.py:255
  38.6 2.0 %collective-permute-start.3 = (bf16[528,512]{1,0:T(8,128)(2,1)S(1)}, bf16[528,512]{1,0:T(8,128)(2,1)S(1)}, u32[]{:S(2)}, u32[]{:S(2)}) collective-permute-start(bf16[528,512]{1,0:T(8,128)(2,1)S(1)} %add_add_fusion), channel_id=1, source_target_pairs={{0,1},{1,0},{2,3},{3,2},{4,5},{5,4},{6,7},{7,6},{8,9},{9,8},{10,11... | collective-permute-start | bytes 1622024 | tf_op jit(solution)/shard_map/ppermute | solution.py:241
  40.8 0.8 copy-start.1
  41.6 0.8 copy-start.3
  45.4 13.2 %copy-start.2 = (bf16[512,512]{1,0:T(8,128)(2,1)S(1)}, bf16[512,512]{1,0:T(8,128)(2,1)}, u32[]{:S(2)}) copy-start(bf16[512,512]{1,0:T(8,128)(2,1)} %copy-done.1) | copy-start | bytes 1572868
  45.4 13.2 %copy-start.4 = (bf16[512,512]{1,0:T(8,128)(2,1)S(1)}, bf16[512,512]{1,0:T(8,128)(2,1)}, u32[]{:S(2)}) copy-start(bf16[512,512]{1,0:T(8,128)(2,1)} %copy-done.3) | copy-start | bytes 1572868

commit v2 on v1

v2 whole, which is shorter than its diff:
```python
import functools

import jax
import jax.numpy as jnp
import numpy as np
from jax import lax
from jax.experimental import pallas as pl
from jax.experimental.pallas import tpu as pltpu
from jax.sharding import PartitionSpec as P

ROTS = 16
SHARPNESS = 2.0
RIDGE = 0.1
BIG = 256
SMALL = 128
TAIL = 16
VMEM_BYTES = 60 * 2**20
F32, BF16 = jnp.float32, jnp.bfloat16


def split(x):
    hi = x.astype(BF16)
    return hi, (x - hi.astype(F32)).astype(BF16)


def dot_nt(a, b):
    return lax.dot_general(a, b, (((1,), (1,)), ((), ())), preferred_element_type=F32)


def dot_nn(a, b):
    return jnp.dot(a, b, preferred_element_type=F32)


def dot3(dot, ah, al, bh, bl):
    return dot(ah, bh) + (dot(ah, bl) + dot(al, bh))


def gauss_jordan(rows):
    groups = len(rows)
    shape = (8, SMALL)
    sub = lax.broadcasted_iota(jnp.int32, shape, 0)
    lane = lax.broadcasted_iota(jnp.int32, shape, 1)
    left = list(rows)
    right = [jnp.where(sub + 8 * g == lane, 1.0, 0.0).astype(F32) for g in range(groups)]
    out = []
    for g in range(groups):
        a, b = left[g], right[g]
        cols = [jnp.broadcast_to(a[:, 8 * g + k : 8 * g + k + 1], shape) for k in range(8)]
        kept = jnp.zeros(shape, F32)
        for k in range(8):
            pivot = jnp.broadcast_to(cols[k][k : k + 1, :], shape)
            inv = 1.0 / pivot
            mult = jnp.where(sub == k, 1.0 - inv, cols[k] * inv)
            arow = jnp.broadcast_to(a[k : k + 1, :], shape)
            brow = jnp.broadcast_to(b[k : k + 1, :], shape)
            kept = jnp.where(sub == k, brow * lax.rsqrt(pivot), kept)
            a = a - mult * arow
            b = b - mult * brow
            for j in range(k + 1, 8):
                cols[j] = cols[j] - mult * jnp.broadcast_to(cols[j][k : k + 1, :], shape)
        out.append(kept)
        for i in range(g + 1, groups):
            suma = sumb = None
            for k in range(8):
                c = jnp.broadcast_to(left[i][:, 8 * g + k : 8 * g + k + 1], shape)
                ta = c * jnp.broadcast_to(a[k : k + 1, :], shape)
                tb = c * jnp.broadcast_to(b[k : k + 1, :], shape)
                suma, sumb = (ta, tb) if suma is None else (suma + ta, sumb + tb)
            left[i] = left[i] - suma
            right[i] = right[i] - sumb
    return out


def iota(n, axis):
    shape = (n, 1) if axis == 0 else (1, n)
    return lax.broadcasted_iota(jnp.int32, shape, axis)


def ridge(row_ids, col_ids):
    return jnp.where(row_ids == col_ids, RIDGE, 0.0).astype(F32)


def al(v, m):
    return pl.multiple_of(v, m)


def evaluate(acc_ref, x_ref, row0, tm, t_ref, li_ref, xi_ref, col0, tn):
    feat = x_ref.shape[1]
    chan = feat // ROTS
    acc = acc_ref.at[0:tm, 0:tn]
    for s in range(ROTS):
        w = t_ref[feat - chan * s : 2 * feat - chan * s, pl.ds(col0, tn)]
        e = jnp.exp(dot_nn(x_ref[pl.ds(row0, tm), :], w))
        acc[...] = e if s == 0 else acc[...] + e
    af = x_ref[pl.ds(row0, tm), :].astype(F32)
    rn = jnp.sum(af * af, axis=1, keepdims=True) * (1.0 / feat) + SHARPNESS
    info = xi_ref[pl.ds(row0, tm), :]
    cc, cs, cn = (li_ref[k : k + 1, pl.ds(col0, tn)] for k in range(3))
    arg = info[:, 0:1] * cc + info[:, 1:2] * cs - rn - cn
    return acc[...] * jnp.exp(arg) * (1.0 / ROTS)


def unpack_rows(block_rows, block_cols, q, got_ref, swap_ref, x_ref, b_ref, groups, row0):
    half = block_rows // 2
    tail = half + block_cols
    for n, c in enumerate(groups):
        at = row0 + n * block_rows
        mine, theirs = (al(at + ((q % 2) ^ k) * half, half) for k in range(2))
        x_ref[pl.ds(mine, half), :] = got_ref[c, 0:half, :]
        x_ref[pl.ds(theirs, half), :] = swap_ref[c, :, :]
        b_ref[0:1, at : at + block_rows] = got_ref[c, tail : tail + 1, 0:block_rows].astype(F32)


def unpack_cols(block_rows, block_cols, got_ref, x_ref, b_ref, row0):
    half = block_rows // 2
    tail = half + block_cols
    for n in range(got_ref.shape[0] - 1):
        at = row0 + n * block_cols
        x_ref[at : at + block_cols, :] = got_ref[n + 1, half:tail, :]
        bins = got_ref[n + 1, tail : tail + 1, block_rows : block_rows + block_cols]
        b_ref[0:1, at : at + block_cols] = bins.astype(F32)


def spread_info(x_ref, t_ref, b_ref, flip_ref, xi_ref, li_ref, col0, cols):
    feat = x_ref.shape[1]
    rows = x_ref.shape[0]
    bins = b_ref[0:1, :]
    cos, sin = jnp.zeros_like(bins), jnp.zeros_like(bins)
    for v in range(ROTS):
        hit = bins == float(v)
        cos = jnp.where(hit, float(np.cos(2.0 * np.pi * v / ROTS)), cos)
        sin = jnp.where(hit, float(np.sin(2.0 * np.pi * v / ROTS)), sin)
    flip_ref[0:1, :] = SHARPNESS * cos
    flip_ref[1:2, :] = SHARPNESS * sin
    for n in range(rows // SMALL):
        at = slice(n * SMALL, (n + 1) * SMALL)
        xi_ref[at, :] = flip_ref[:, at].T
    li_ref[0:1, :] = cos[:, col0 : col0 + cols]
    li_ref[1:2, :] = sin[:, col0 : col0 + cols]
    eye = jnp.where(iota(feat, 0) == iota(feat, 1), 1.0 / 256.0, 0.0).astype(BF16)
    for n in range(cols // SMALL):
        at = slice(n * SMALL, (n + 1) * SMALL)
        t = dot_nt(eye, x_ref[col0 + n * SMALL : col0 + (n + 1) * SMALL, :])
        li_ref[2:3, at] = jnp.sum(t * t, axis=0, keepdims=True) * (256.0 * 256.0 / feat)
        t = t.astype(BF16)
        t_ref[0:feat, at] = t
        t_ref[feat : 2 * feat, at] = t


def pack_kernel(pq_ref, pool_ref, ids_ref, bins_ref, col_bins_ref, out_ref, lead_ref, f_ref, flip_ref):
    q = pq_ref[1]
    lead, feat = pool_ref.shape
    groups, rows, _ = out_ref.shape
    block_rows = lead // groups
    half = block_rows // 2
    block_cols = rows - half - TAIL
    quarter = lead // 4
    flip_ref[0:1, :] = ids_ref[...].astype(F32)
    for n in range(lead // SMALL):
        at = slice(n * SMALL, (n + 1) * SMALL)
        ids = flip_ref[:, at].T[:, 0:1].astype(jnp.int32)
        hot = jnp.where(ids == iota(lead, 1), 1.0, 0.0).astype(BF16)
        f_ref[at, :] = dot_nn(hot, pool_ref[...]).astype(BF16)
    bins = bins_ref[...].astype(F32)
    flip_ref[0:1, :] = bins
    piece = f_ref[pl.ds(al(q * block_cols, block_cols), block_cols), :]
    for r in range(groups):
        out_ref[r, 0:half, :] = f_ref[pl.ds(al(r * block_rows + (q % 2) * half, half), half), :]
        out_ref[r, half : half + block_cols, :] = piece
        tail = jnp.concatenate(
            [bins[:, r * block_rows : (r + 1) * block_rows], col_bins_ref[...].astype(F32)], axis=1)
        tail = jnp.pad(tail, ((0, TAIL - 1), (0, feat - tail.shape[1])))
        out_ref[r, half + block_cols :, :] = tail.astype(BF16)
    at = pl.ds(al((q % 4) * quarter, quarter), quarter)
    lead_ref[0:quarter, :] = f_ref[at, :]
    tail = jnp.pad(flip_ref[0:1, at], ((0, TAIL - 1), (0, feat - quarter)))
    lead_ref[quarter:, :] = tail.astype(BF16)


def trail_kernel(block_rows, block_cols, lead, pq_ref, got_ref, swap_ref, out_ref, x_ref, t_ref, b_ref, flip_ref, xi_ref, li_ref, *acc_refs):
    p, q = pq_ref[0], pq_ref[1]
    groups = got_ref.shape[0]
    own = groups * block_rows
    cols = (groups - 1) * block_cols
    cols_pad = out_ref.shape[1]
    b_ref[...] = jnp.zeros(b_ref.shape, F32)
    unpack_rows(block_rows, block_cols, q, got_ref, swap_ref, x_ref, b_ref, range(groups), 0)
    unpack_cols(block_rows, block_cols, got_ref, x_ref, b_ref, own)
    if cols < cols_pad:
        x_ref[own + cols :, :] = jnp.zeros((cols_pad - cols, x_ref.shape[1]), BF16)
    spread_info(x_ref, t_ref, b_ref, flip_ref, xi_ref, li_ref, own, cols_pad)
    lane = iota(cols_pad, 1)
    col_ids = (lane // block_cols + 1) * lead + q * block_cols + lane % block_cols

    def tile(n, _):
        for u in range(len(acc_refs)):
            c = n * len(acc_refs) + u
            row0 = al(c * block_rows, block_rows)
            v = evaluate(acc_refs[u], x_ref, row0, block_rows, t_ref, li_ref, xi_ref, 0, cols_pad)
            row_ids = c * lead + p * block_rows + iota(block_rows, 0)
            out_ref[pl.ds(row0, block_rows), :] = v + ridge(row_ids, col_ids)
        return 0
    lax.fori_loop(0, groups // len(acc_refs), tile, 0)


def panel_kernel(dims, jobs_ref, pq_ref, q0_ref, q1_ref, q2_ref, q3_ref, got_ref, swap_ref, k_ref, trail_out, *refs):
    lead, other, block_rows, block_cols, tile_other = dims
    width = block_cols if block_cols % SMALL == 0 else None
    if width is None:
        lead_out, *refs = refs
    s_ref, ph_ref, pl_ref, d_ref, x32_ref, x_ref, lt_ref, b_ref, flip_ref, xi_ref, li_ref, *acc_refs = refs
    feat = x_ref.shape[1]
    nbig = lead // BIG
    others = other // tile_other
    groups = got_ref.shape[0]
    half = block_rows // 2
    rows_other = (groups - 1) * block_rows
    cols_pad = other - rows_other
    p, q = pq_ref[0], pq_ref[1]

    first = al(p * block_rows, block_rows)

    def lead_tile(acc_ref, row0, col0, scale=None):
        v = evaluate(acc_ref, x_ref, row0, BIG, lt_ref, li_ref, xi_ref, col0, BIG)
        v = v + ridge(row0 + iota(BIG, 0), col0 + iota(BIG, 1))
        at = (pl.ds(row0, BIG), pl.ds(col0, BIG))
        s_ref[at] = s_ref[at] + (v if scale is None else v * scale)

    def lead_job(acc_ref, n):
        row0, col0 = al(jobs_ref[3 * n], BIG), al(jobs_ref[3 * n + 1], BIG)
        lead_tile(acc_ref, row0, col0, jobs_ref[3 * n + 2].astype(F32))

    def other_tile(acc_ref, i, j):
        row0, col0 = lead + i * tile_other, al(j * BIG, BIG)
        at = (pl.ds(row0, tile_other), pl.ds(col0, BIG))
        s_ref[at] = s_ref[at] + evaluate(
            acc_ref, x_ref, row0, tile_other, lt_ref, li_ref, xi_ref, col0, BIG)

    def own_row(c):
        return al(jnp.where(c == 0, first, lead + (c - 1) * block_rows), SMALL)

    left = 0 if width is None else width

    quarter = lead // 4
    b_ref[...] = jnp.zeros(b_ref.shape, F32)
    for ref, flip in ((q0_ref, 0), (q1_ref, 1), (q2_ref, 2), (q3_ref, 3)):
        at = al(((q % 4) ^ flip) * quarter, quarter)
        x_ref[pl.ds(at, quarter), :] = ref[0:quarter, :]
        b_ref[0:1, pl.ds(at, quarter)] = ref[quarter : quarter + 1, 0:quarter].astype(F32)
    unpack_rows(block_rows, block_cols, q, got_ref, swap_ref, x_ref, b_ref, range(1, groups), lead)
    unpack_cols(block_rows, block_cols, got_ref, x_ref, b_ref, lead + rows_other)
    if (groups - 1) * block_cols < cols_pad:
        at = lead + rows_other + (groups - 1) * block_cols
        x_ref[at:, :] = jnp.zeros((lead + other - at, feat), BF16)
    spread_info(x_ref, lt_ref, b_ref, flip_ref, xi_ref, li_ref, 0, lead)

    def clear(i, _):
        at = pl.ds(al(i * SMALL, SMALL), SMALL)
        s_ref[at, :] = jnp.zeros((SMALL, lead), F32)
        ph_ref[at, :] = jnp.zeros((SMALL, lead), BF16)
        pl_ref[at, :] = jnp.zeros((SMALL, lead), BF16)
        return 0
    lax.fori_loop(0, (lead + other) // SMALL, clear, 0)
    lead_tile(acc_refs[0], 0, 0)
    lead_tile(acc_refs[1], BIG, 0)

    def invert(r0):
        rows = [d_ref[r0 + 8 * g : r0 + 8 * g + 8, r0 : r0 + SMALL] for g in range(SMALL // 8)]
        for g, v in enumerate(gauss_jordan(rows)):
            x32_ref[r0 + 8 * g : r0 + 8 * g + 8, r0 : r0 + SMALL] = v

    def big_step(j, last):
        c0 = al(j * BIG, BIG)
        cj = pl.ds(c0, BIG)
        work = [functools.partial(other_tile, i=i, j=j) for i in range(others)]
        if not last:
            work[others - 1 : others - 1] = [
                functools.partial(lead_job, n=j * (nbig - 1) + u) for u in range(nbig - 1)]
        cut = -(-len(work) // 2)
        d_ref[...] = s_ref[cj, cj]
        invert(0)
        for n, job in enumerate(work[:cut]):
            job(acc_refs[n % len(acc_refs)])
        x11 = split(x32_ref[0:SMALL, 0:SMALL])
        l21 = split(dot3(dot_nt, *split(d_ref[SMALL:, 0:SMALL]), *x11))
        d_ref[SMALL:, SMALL:] = d_ref[SMALL:, SMALL:] - dot3(dot_nt, *l21, *l21)
        invert(SMALL)
        mid = split(dot3(dot_nn, *l21, *x11))
        for n, job in enumerate(work[cut:]):
            job(acc_refs[n % len(acc_refs)])
        x22 = split(x32_ref[SMALL:, SMALL:])
        x32_ref[SMALL:, 0:SMALL] = -dot3(dot_nn, *x22, *mid)
        x32_ref[0:SMALL, SMALL:] = jnp.zeros((SMALL, SMALL), F32)
        xh, xl = split(x32_ref[...])

        def solve(r0, tm, mask):
            v = dot3(dot_nt, *split(s_ref[pl.ds(r0, tm), cj]), xh, xl)
            if mask:
                keep = lax.broadcasted_iota(jnp.int32, v.shape, 0) >= lax.broadcasted_iota(jnp.int32, v.shape, 1)
                v = jnp.where(keep, v, 0.0)
            s_ref[pl.ds(r0, tm), cj] = v
            h, l = split(v)
            ph_ref[pl.ds(r0, tm), cj] = h
            pl_ref[pl.ds(r0, tm), cj] = l

        solve(c0, BIG, True)
        if not last:
            def lead_solve(i, _):
                solve(al(i * BIG, BIG), BIG, False)
                return 0
            lax.fori_loop(j + 1, nbig, lead_solve, 0)
        def other_solve(i, _):
            solve(al(lead + i * tile_other, SMALL), tile_other, False)
            return 0
        lax.fori_loop(0, others, other_solve, 0)
        if last:
            return

        def update(r0, tm, k0):
            kj = pl.ds(k0, BIG)
            rows = pl.ds(r0, tm)
            s_ref[rows, kj] = s_ref[rows, kj] - dot3(
                dot_nt, ph_ref[rows, cj], pl_ref[rows, cj], ph_ref[kj, cj], pl_ref[kj, cj])

        def update_col(k, _):
            k0 = al(k * BIG, BIG)
            def lead_update(i, _):
                update(al(i * BIG, BIG), BIG, k0)
                return 0
            lax.fori_loop(k, nbig, lead_update, 0)
            def other_update(i, _):
                update(al(lead + i * tile_other, SMALL), tile_other, k0)
                return 0
            lax.fori_loop(0, others, other_update, 0)
            return 0
        lax.fori_loop(j + 1, nbig, update_col, 0)

    def loop_step(j, _):
        big_step(j, False)
        return 0
    lax.fori_loop(0, nbig - 1, loop_step, 0)
    big_step(nbig - 1, True)

    cols0 = lead + rows_other

    def trailing(c, _):
        rows = pl.ds(own_row(c), block_rows)
        at = pl.ds(al(c * block_rows, block_rows), block_rows)
        trail_out[at, left:] = k_ref[at, :] - dot3(
            dot_nt, ph_ref[rows, :], pl_ref[rows, :],
            ph_ref[cols0 : cols0 + cols_pad, :], pl_ref[cols0 : cols0 + cols_pad, :])
        if width is None:
            lead_out[at, :] = s_ref[rows, :]
        else:
            trail_out[at, 0:width] = s_ref[rows, pl.ds(al(q * width, width), width)]
        return 0
    lax.fori_loop(0, groups, trailing, 0)


def job_table(nbig):
    table = []
    for t in range(nbig - 1):
        tiles = [(i, t) for i in range(t + 1, nbig)] + [(t + 1, t + 1)]
        tiles = tiles[1:] if t == 0 else tiles
        tiles = [(i * BIG, j * BIG, 1) for i, j in tiles]
        table += tiles + [(0, 0, 0)] * (nbig - 1 - len(tiles))
    return np.array(table, np.int32).reshape(-1)


def per_device(replay_pool, sample_ids, rotation_bins):
    rows_n = lax.axis_size("row")
    cols_n = lax.axis_size("col")
    p = lax.axis_index("row")
    q = lax.axis_index("col")
    lead, feat = replay_pool.shape
    block_rows = lead // rows_n
    block_cols = lead // cols_n
    rows_other = (rows_n - 1) * block_rows
    cols_other = (rows_n - 1) * block_cols
    cols_pad = -(-cols_other // SMALL) * SMALL
    other = rows_other + cols_pad
    total = lead + other
    own = rows_n * block_rows
    half = block_rows // 2
    tile_other = max(t for t in range(SMALL, 513, SMALL) if other % t == 0)
    aligned = block_cols % SMALL == 0
    smem = pl.BlockSpec(memory_space=pltpu.SMEM)
    vmem = pl.BlockSpec(memory_space=pltpu.VMEM)
    params = pltpu.CompilerParams(vmem_limit_bytes=VMEM_BYTES)
    pq = jnp.stack([p, q]).astype(jnp.int32)

    def shape(*dims, dtype=F32):
        return jax.ShapeDtypeStruct(dims, dtype)

    message, quarter = pl.pallas_call(
        pack_kernel,
        out_shape=(shape(rows_n, half + block_cols + TAIL, feat, dtype=BF16), shape(lead // 4 + TAIL, feat, dtype=BF16)),
        in_specs=[smem] + [vmem] * 4,
        out_specs=(vmem, vmem),
        scratch_shapes=[pltpu.VMEM((lead, feat), BF16), pltpu.VMEM((SMALL, lead), F32)],
        compiler_params=params,
        name="pack",
    )(pq, replay_pool, sample_ids, rotation_bins[None],
      lax.dynamic_slice_in_dim(rotation_bins, q * block_cols, block_cols, 0)[None])

    got = lax.all_to_all(message, "row", split_axis=0, concat_axis=0)
    swap = lax.ppermute(got[:, :half], "col", [(i, i ^ 1) for i in range(cols_n)])

    mine = jnp.where(p == 0, quarter, jnp.zeros_like(quarter))
    for d in range(1, rows_n):
        mine = mine + lax.ppermute(quarter, "row", [(0, d)])
    over_z = lax.ppermute(mine, "col", [(i, i ^ 2) for i in range(cols_n)])
    sibling = lax.ppermute(mine, "col", [(i, i ^ 1) for i in range(cols_n)])
    both = lax.ppermute(over_z, "col", [(i, i ^ 1) for i in range(cols_n)])

    trailing = pl.pallas_call(
        functools.partial(trail_kernel, block_rows, block_cols, lead),
        out_shape=shape(own, cols_pad),
        in_specs=[smem] + [vmem] * 2,
        out_specs=vmem,
        scratch_shapes=[
            pltpu.VMEM((own + cols_pad, feat), BF16),
            pltpu.VMEM((2 * feat, cols_pad), BF16),
            pltpu.VMEM((8, own + cols_pad), F32),
            pltpu.VMEM((SMALL, own + cols_pad), F32),
            pltpu.VMEM((own + cols_pad, SMALL), F32),
            pltpu.VMEM((8, cols_pad), F32),
        ] + [pltpu.VMEM((block_rows, cols_pad), F32)] * 2,
        compiler_params=params,
        cost_estimate=pl.CostEstimate(
            flops=2 * ROTS * own * cols_pad * feat, bytes_accessed=8 * own * cols_pad, transcendentals=0),
        name="trail",
    )(pq, got, swap)

    shapes = [shape(own, cols_pad + (block_cols if aligned else 0))]
    if not aligned:
        shapes.append(shape(own, lead))
    tile, *lead_out = pl.pallas_call(
        functools.partial(panel_kernel, (lead, other, block_rows, block_cols, tile_other)),
        out_shape=shapes,
        in_specs=[smem] * 2 + [vmem] * 7,
        out_specs=[vmem] * len(shapes),
        scratch_shapes=[
            pltpu.VMEM((total, lead), F32),
            pltpu.VMEM((total, lead), BF16),
            pltpu.VMEM((total, lead), BF16),
            pltpu.VMEM((BIG, BIG), F32),
            pltpu.VMEM((BIG, BIG), F32),
            pltpu.VMEM((total, feat), BF16),
            pltpu.VMEM((2 * feat, lead), BF16),
            pltpu.VMEM((8, total), F32),
            pltpu.VMEM((SMALL, total), F32),
            pltpu.VMEM((total, SMALL), F32),
            pltpu.VMEM((8, lead), F32),
        ] + [pltpu.VMEM((max(BIG, tile_other), BIG), F32)] * 4,
        compiler_params=params,
        name="panel",
    )(jnp.asarray(job_table(lead // BIG)), pq, mine, sibling, over_z, both, got, swap, trailing)
    if aligned:
        return tile
    leading = lax.dynamic_slice_in_dim(lead_out[0], q * block_cols, block_cols, 1)
    return jnp.concatenate([leading, tile[:, :cols_other]], axis=1)


def solution(mesh):
    in_specs = (P("row", None), P("row", None), P("row"))
    return jax.shard_map(per_device, mesh=mesh, in_specs=in_specs, out_specs=P("row", "col"), check_vma=False)
```

time: 176 us -> 134 us (0.76)
  Pallas kernels: 113 us -> 92.1 us
  local copies, waits for them, and re-layouts: 14.9 us -> 3.56 us
  other arithmetic: 8.67 us -> 0.7 us
  waiting for transfers between devices: 24.5 us -> 22.4 us
    pallas_call x1 -> x3, Pallas kernels: 113 us -> 92.1 us  [the longest x1 75.5 us: per_device(): pl.pallas_call(functools.partial(panel_kernel, (lead, other, block_rows,...]
    concatenate x6 -> x0, other arithmetic: 4.07 us -> none  [the longest x1 1.51 us: per_device(): x = jnp.concatenate([lead_feats, row_feats, col_feats])]
    gather x1 -> x0, local copies, waits for them, and re-layouts: 3.97 us -> none  [per_device(): features = replay_pool[sample_ids[0]]]
    slice x9 -> x1, local copies, waits for them, and re-layouts: 3.51 us -> 0.04 us  [per_device(): got[:, :half]]
    concatenate x2 -> x0, local copies, waits for them, and re-layouts: 2.65 us -> none  [the longest x1 2.58 us: per_device(): lt = jnp.concatenate([lt, lt])]
    ppermute x4 -> x7, waiting for transfers between devices: 16.4 us -> 15.5 us  [the longest x3 9.61 us: per_device(): mine = mine + lax.ppermute(quarter, 'row', [(0, d)])]
    ppermute x4 -> x7, starting transfers between devices: 9.98 us -> 9.23 us  [the longest x3 7.45 us: per_device(): mine = mine + lax.ppermute(quarter, 'row', [(0, d)])]
  transfers between devices with their start and end apart: 5 -> 8, of which waited for: 5 -> 4; matrix products, arithmetic and copies ran while one was open for 4% -> 0% of each run, Pallas kernels for 0% -> 10%
where the time goes in v2:
time: 134 us; the launch traced here: 133 us
  Pallas kernels  92.1 us (69%)
  waiting for transfers between devices  22.4 us (17%)
  starting transfers between devices  14.6 us (11%)
  local copies, waits for them, and re-layouts  3.56 us (3%)
    pallas_call x1, Pallas kernels, per_device(): pl.pallas_call(functools.partial(panel_kernel, (lead, other, block_rows,...  75.5 us
    pallas_call x1, Pallas kernels, per_device(): pl.pallas_call(functools.partial(trail_kernel, block_rows, block_cols, le...  12.8 us
    ppermute x3, waiting for transfers between devices, per_device(): mine = mine + lax.ppermute(quarter, 'row', [(0, d)])  9.61 us
    ppermute x3, starting transfers between devices, per_device(): mine = mine + lax.ppermute(quarter, 'row', [(0, d)])  7.45 us
    all_to_all x1, waiting for transfers between devices, per_device(): got = lax.all_to_all(message, 'row', split_axis=0, concat_axis=0)  6.87 us
    ppermute x1, waiting for transfers between devices, per_device(): over_z = lax.ppermute(mine, 'col', [(i, i ^ 2) for i in range(cols_n)])  5.91 us
    all_to_all x1, starting transfers between devices, per_device(): got = lax.all_to_all(message, 'row', split_axis=0, concat_axis=0)  5.32 us
    pallas_call x1, Pallas kernels, per_device(): pl.pallas_call(pack_kernel, out_shape=(shape(rows_n, half + block_cols +...  3.76 us
  transfers between devices with their start and end apart: 8, of which 4 were waited for; matrix products, arithmetic and copies ran while one was open for 0% of the time, Pallas kernels for 10%

profile of v2, /device:TPU:0, one launch (start us, length us, event | category | flops | bytes accessed | tf_op | source)
XLA Modules:
  0.0 133.4 jit_solution(16478456096012105576)
XLA Ops:
  0.0 0.6 pad_add_fusion.pq_ref
  0.6 1.3 dynamic-slice_bitcast_fusion.col_bins_ref
  1.9 3.8 %pack.1 = (bf16[4,272,512]{2,1,0:T(8,128)(2,1)}, bf16[272,512]{1,0:T(8,128)(2,1)}) custom-call(s32[2]{0:T(128)} %pad_add_fusion.pq_ref, bf16[1024,512]{1,0:T(8,128)(2,1)} %pool_ref.1, s32[1,1024]{1,0:T(1,128)} %ids_ref.1, s32[1,1024]{1,0:T(1,128)} %bitcast.5, s32[1,128]{1,0:T(1,128)} %dynamic-slice_bitcast_fusion.col_bins_ref), custom_call_target="tpu_custom_call" | custom-call | tf_op jit(solution)/shard_map/pack/pallas_call | solution.py:395
  5.7 5.3 %all-to-all-start = ((bf16[4,272,512]{2,1,0:T(8,128)(2,1)}), bf16[4,272,512]{2,1,0:T(8,128)(2,1)S(1)}, u32[]{:S(2)}, u32[]{:S(2)}) async-start(bf16[4,272,512]{2,1,0:T(8,128)(2,1)} %get-tuple-element.8), calls=%async_computation | async-start | bytes 2228224 | tf_op jit(solution)/shard_map/all_to_all | solution.py:406
  11.0 0.0 copy-done.3
  11.0 4.8 %collective-permute-start.2 = (bf16[272,512]{1,0:T(8,128)(2,1)S(1)}, bf16[272,512]{1,0:T(8,128)(2,1)S(1)}, u32[]{:S(2)}, u32[]{:S(2)}) collective-permute-start(bf16[272,512]{1,0:T(8,128)(2,1)S(1)} %copy-done.3), channel_id=1, source_target_pairs={{0,24},{1,25},{2,26},{3,27},{4,28},{5,29},{6,30},{7,31}} | collective-permute-start | bytes 835592 | tf_op jit(solution)/shard_map/ppermute | solution.py:411
  15.9 1.3 collective-permute-start.1
  17.2 1.3 collective-permute-start
  18.5 6.9 %all-to-all-done.got_ref = bf16[4,272,512]{2,1,0:T(8,128)(2,1)S(1)} async-done(((bf16[4,272,512]{2,1,0:T(8,128)(2,1)}), bf16[4,272,512]{2,1,0:T(8,128)(2,1)S(1)}, u32[]{:S(2)}, u32[]{:S(2)}) %all-to-all-start) | async-done | bytes 1114144 | tf_op jit(solution)/shard_map/all_to_all | solution.py:406
  25.4 0.1 collective-permute-start.6
  25.5 4.8 %collective-permute-done.2 = bf16[272,512]{1,0:T(8,128)(2,1)S(1)} collective-permute-done((bf16[272,512]{1,0:T(8,128)(2,1)S(1)}, bf16[272,512]{1,0:T(8,128)(2,1)S(1)}, u32[]{:S(2)}, u32[]{:S(2)}) %collective-permute-start.2) | collective-permute-done | bytes 278560 | tf_op jit(solution)/shard_map/ppermute | solution.py:411
  30.3 0.0 collective-permute-done.1
  30.3 4.8 %collective-permute-done = bf16[272,512]{1,0:T(8,128)(2,1)S(1)} collective-permute-done((bf16[272,512]{1,0:T(8,128)(2,1)S(1)}, bf16[272,512]{1,0:T(8,128)(2,1)S(1)}, u32[]{:S(2)}, u32[]{:S(2)}) %collective-permute-start) | collective-permute-done | bytes 278560 | tf_op jit(solution)/shard_map/ppermute | solution.py:411
  35.1 0.1 add_add_fusion.q0_ref
  35.2 0.0 copy-start.1
  35.2 1.7 %collective-permute-start.4 = (bf16[272,512]{1,0:T(8,128)(2,1)S(1)}, bf16[272,512]{1,0:T(8,128)(2,1)S(1)}, u32[]{:S(2)}, u32[]{:S(2)}) collective-permute-start(bf16[272,512]{1,0:T(8,128)(2,1)S(1)} %add_add_fusion.q0_ref), channel_id=1, source_target_pairs={{0,2},{1,3},{2,0},{3,1},{4,6},{5,7},{6,4},{7,5},{8,10},{9,11},{10,... | collective-permute-start | bytes 835592 | tf_op jit(solution)/shard_map/ppermute | solution.py:412
  36.9 0.0 collective-permute-start.3
  36.9 5.9 %collective-permute-done.4.q2_ref = bf16[272,512]{1,0:T(8,128)(2,1)S(1)} collective-permute-done((bf16[272,512]{1,0:T(8,128)(2,1)S(1)}, bf16[272,512]{1,0:T(8,128)(2,1)S(1)}, u32[]{:S(2)}, u32[]{:S(2)}) %collective-permute-start.4) | collective-permute-done | bytes 278560 | tf_op jit(solution)/shard_map/ppermute | solution.py:412
  42.8 0.0 collective-permute-start.5
  42.8 0.0 collective-permute-done.6.swap_ref
  42.8 0.0 copy-done
  42.8 0.0 copy-start.2
  42.8 0.8 copy-done.2
  43.7 12.8 %trail.1.k_ref = f32[1024,384]{1,0:T(8,128)} custom-call(s32[2]{0:T(128)} %pad_add_fusion.pq_ref, bf16[4,272,512]{2,1,0:T(8,128)(2,1)} %copy-done, bf16[4,128,512]{2,1,0:T(8,128)(2,1)} %copy-done.2), custom_call_target="tpu_custom_call" | custom-call | flops 6442450944 | bytes 3145728 | tf_op jit(solution)/shard_map/trail/pallas_call | solution.py:416
  56.5 0.0 copy-done.1
  56.5 0.0 copy-done.4
  56.5 0.0 collective-permute-done.3.q1_ref
  56.5 0.0 copy-start.5
  56.5 0.0 collective-permute-done.5.q3_ref
  56.5 0.7 copy-done.5
  57.2 0.7 copy-done.6
  57.9 75.5 %panel.1 = f32[1024,512]{1,0:T(8,128)} custom-call(s32[27]{0:T(128)} %constant.18.clone.jobs_ref, s32[2]{0:T(128)} %pad_add_fusion.pq_ref, bf16[272,512]{1,0:T(8,128)(2,1)} %copy-done.1, bf16[272,512]{1,0:T(8,128)(2,1)} %copy-done.5, bf16[272,512]{1,0:T(8,128)(2,1)} %copy-done.4, bf16[272,512]{1,0:T(8,128)(2,1)} %copy-done.6, bf16[4,272,512]{2,1,0:T(8,128)(2,1)} %copy-done, ...), custom_call_target="tpu_custom_call" | custom-call | tf_op jit(solution)/shard_map/panel/pallas_call | solution.py:438
  (5 shorter events, 0.0 us)
Async XLA Ops:
  5.7 5.3 %copy-start.3 = (bf16[272,512]{1,0:T(8,128)(2,1)S(1)}, bf16[272,512]{1,0:T(8,128)(2,1)}, u32[]{:S(2)}) copy-start(bf16[272,512]{1,0:T(8,128)(2,1)} %get-tuple-element.7) | copy-start | bytes 835588
  5.7 19.7 %all-to-all-start = ((bf16[4,272,512]{2,1,0:T(8,128)(2,1)}), bf16[4,272,512]{2,1,0:T(8,128)(2,1)S(1)}, u32[]{:S(2)}, u32[]{:S(2)}) async-start(bf16[4,272,512]{2,1,0:T(8,128)(2,1)} %get-tuple-element.8), calls=%async_computation | async-start | bytes 2228224 | tf_op jit(solution)/shard_map/all_to_all | solution.py:406
  11.0 19.2 %collective-permute-start.2 = (bf16[272,512]{1,0:T(8,128)(2,1)S(1)}, bf16[272,512]{1,0:T(8,128)(2,1)S(1)}, u32[]{:S(2)}, u32[]{:S(2)}) collective-permute-start(bf16[272,512]{1,0:T(8,128)(2,1)S(1)} %copy-done.3), channel_id=1, source_target_pairs={{0,24},{1,25},{2,26},{3,27},{4,28},{5,29},{6,30},{7,31}} | collective-permute-start | bytes 835592 | tf_op jit(solution)/shard_map/ppermute | solution.py:411
  15.9 14.4 %collective-permute-start.1 = (bf16[272,512]{1,0:T(8,128)(2,1)S(1)}, bf16[272,512]{1,0:T(8,128)(2,1)S(1)}, u32[]{:S(2)}, u32[]{:S(2)}) collective-permute-start(bf16[272,512]{1,0:T(8,128)(2,1)S(1)} %copy-done.3), channel_id=1, source_target_pairs={{0,16},{1,17},{2,18},{3,19},{4,20},{5,21},{6,22},{7,23}} | collective-permute-start | bytes 835592 | tf_op jit(solution)/shard_map/ppermute | solution.py:411
  17.2 17.9 %collective-permute-start = (bf16[272,512]{1,0:T(8,128)(2,1)S(1)}, bf16[272,512]{1,0:T(8,128)(2,1)S(1)}, u32[]{:S(2)}, u32[]{:S(2)}) collective-permute-start(bf16[272,512]{1,0:T(8,128)(2,1)S(1)} %copy-done.3), channel_id=1, source_target_pairs={{0,8},{1,9},{2,10},{3,11},{4,12},{5,13},{6,14},{7,15}} | collective-permute-start | bytes 835592 | tf_op jit(solution)/shard_map/ppermute | solution.py:411
  25.4 17.4 %copy-start = (bf16[4,272,512]{2,1,0:T(8,128)(2,1)}, bf16[4,272,512]{2,1,0:T(8,128)(2,1)S(1)}, u32[]{:S(2)}) copy-start(bf16[4,272,512]{2,1,0:T(8,128)(2,1)S(1)} %all-to-all-done.got_ref) | copy-start | bytes 3342340
  25.4 17.4 %collective-permute-start.6 = (bf16[4,128,512]{2,1,0:T(8,128)(2,1)S(1)}, bf16[4,128,512]{2,1,0:T(8,128)(2,1)S(1)}, u32[]{:S(2)}, u32[]{:S(2)}) collective-permute-start(bf16[4,128,512]{2,1,0:T(8,128)(2,1)S(1)} %slice.4), channel_id=1, source_target_pairs={{0,1},{1,0},{2,3},{3,2},{4,5},{5,4},{6,7},{7,6},{8,9},{9,8},{10,11... | collective-permute-start | bytes 1572872 | tf_op jit(solution)/shard_map/ppermute | solution.py:407
  35.2 21.3 %copy-start.1 = (bf16[272,512]{1,0:T(8,128)(2,1)}, bf16[272,512]{1,0:T(8,128)(2,1)S(1)}, u32[]{:S(2)}) copy-start(bf16[272,512]{1,0:T(8,128)(2,1)S(1)} %add_add_fusion.q0_ref) | copy-start | bytes 835588
  35.2 7.6 %collective-permute-start.4 = (bf16[272,512]{1,0:T(8,128)(2,1)S(1)}, bf16[272,512]{1,0:T(8,128)(2,1)S(1)}, u32[]{:S(2)}, u32[]{:S(2)}) collective-permute-start(bf16[272,512]{1,0:T(8,128)(2,1)S(1)} %add_add_fusion.q0_ref), channel_id=1, source_target_pairs={{0,2},{1,3},{2,0},{3,1},{4,6},{5,7},{6,4},{7,5},{8,10},{9,11},{10,... | collective-permute-start | bytes 835592 | tf_op jit(solution)/shard_map/ppermute | solution.py:412
  36.9 19.6 %collective-permute-start.3 = (bf16[272,512]{1,0:T(8,128)(2,1)S(1)}, bf16[272,512]{1,0:T(8,128)(2,1)S(1)}, u32[]{:S(2)}, u32[]{:S(2)}) collective-permute-start(bf16[272,512]{1,0:T(8,128)(2,1)S(1)} %add_add_fusion.q0_ref), channel_id=1, source_target_pairs={{0,1},{1,0},{2,3},{3,2},{4,5},{5,4},{6,7},{7,6},{8,9},{9,8},{10,11... | collective-permute-start | bytes 835592 | tf_op jit(solution)/shard_map/ppermute | solution.py:413
  42.8 13.7 %copy-start.4 = (bf16[272,512]{1,0:T(8,128)(2,1)}, bf16[272,512]{1,0:T(8,128)(2,1)S(1)}, u32[]{:S(2)}) copy-start(bf16[272,512]{1,0:T(8,128)(2,1)S(1)} %collective-permute-done.4.q2_ref) | copy-start | bytes 835588
  42.8 13.7 %collective-permute-start.5 = (bf16[272,512]{1,0:T(8,128)(2,1)S(1)}, bf16[272,512]{1,0:T(8,128)(2,1)S(1)}, u32[]{:S(2)}, u32[]{:S(2)}) collective-permute-start(bf16[272,512]{1,0:T(8,128)(2,1)S(1)} %collective-permute-done.4.q2_ref), channel_id=1, source_target_pairs={{0,1},{1,0},{2,3},{3,2},{4,5},{5,4},{6,7},{7,6},{8,9},{9,8},{10,11... | collective-permute-start | bytes 835592 | tf_op jit(solution)/shard_map/ppermute | solution.py:414
  42.8 0.8 copy-start.2
  56.5 0.7 copy-start.5
  57.2 0.7 copy-start.6
